TPU v7x, 32 devices: a whole 2x2x4 slice. The times are simulated.
32 devices in a mesh: row: 4 (over z), col: 8 (over y, x, core).
Axes of the slice: x: 2, y: 2, z: 4, core: 2. Of those that a mesh axis runs over, the one named last changes fastest.
Arguments:
- positions: float32 [3, 65536], P(None, ('row', 'col')), may hold values from 0 to 1
- masses: float32 [1, 65536], P(None, ('row', 'col')), may hold values from 2e-09 to 2e-08
- counts: int32 [1, 512], P(None, ('row', 'col')), may hold values from 32 to 128
- sources: int32 [512, 8], P(('row', 'col')), may hold values from 0 to 47, as said below
Outputs:
- accel: float32 [3, 65536], P(None, ('row', 'col'))
Inputs may be any that keep to these rules, and one draw needn't show every extreme that they name: `sources`: each device's source ids name exactly 4 distinct leaves of the lower row neighbour and exactly 4 of the upper one.
All inputs are finite; a program needn't handle non-finite values.
Results may differ from a plain program's by a relative error of at most 0.00024.
Values sent between devices are 32-bit elements; how exact they have to be, the bound alone decides.
A program may use at most 64 MiB of HBM per device.

v0:
```python
import jax
import jax.numpy as jnp
from jax import lax
from jax.sharding import PartitionSpec as P

softening = 2.5e-07


def padded_2(shard, sides, width):
    for axis, dim in sides:
        size, length = (lax.axis_size(axis), shard.shape[dim])
        up = [(i, (i + 1) % size) for i in range(size)]
        down = [(j, i) for i, j in up]
        last = lax.slice_in_dim(shard, length - width, length, axis=dim)
        leading = lax.slice_in_dim(shard, 0, width, axis=dim)
        before = lax.ppermute(last, axis, up)
        after = lax.ppermute(leading, axis, down)
        shard = jnp.concatenate([before, shard, after], axis=dim)
    return shard


def leaf_forces(full_table, targets, sources, alive):
    count = targets.shape[0]
    width = targets.shape[2]
    target_groups = targets.reshape(count // 8, 8, 4, width)
    source_groups = sources.reshape(count // 8, 8, sources.shape[1])
    alive_groups = alive.reshape(count // 8, 8, width)

    def one_group(items):
        target, index, living = items
        source = full_table[index]
        delta_x = source[:, :, 0, None, :] - target[:, None, 0, :, None]
        delta_y = source[:, :, 1, None, :] - target[:, None, 1, :, None]
        delta_z = source[:, :, 2, None, :] - target[:, None, 2, :, None]
        spread = softening + delta_x * delta_x + delta_y * delta_y + delta_z * delta_z
        weight = source[:, :, 3, None, :] / (spread * jnp.sqrt(spread))
        pull_x = jnp.sum(weight * delta_x, axis=(1, 3))
        pull_y = jnp.sum(weight * delta_y, axis=(1, 3))
        pull_z = jnp.sum(weight * delta_z, axis=(1, 3))
        return jnp.stack([pull_x, pull_y, pull_z], axis=1) * living[:, None, :]

    out = lax.map(one_group, (target_groups, source_groups, alive_groups))
    return out.reshape(count, 3, width)


def on_device(positions, masses, counts, sources):
    coords, weights, livecount = (
        lax.all_to_all(positions, "col", split_axis=1, concat_axis=1, tiled=True),
        lax.all_to_all(masses, "col", split_axis=1, concat_axis=1, tiled=True),
        lax.all_to_all(counts, "col", split_axis=1, concat_axis=1, tiled=True),
    )
    leaves = livecount.shape[1]
    width = coords.shape[1] // leaves
    alive = (
        lax.broadcasted_iota(jnp.int32, (leaves, width), 1) < livecount.reshape(leaves, 1)
    ).astype(jnp.float32)
    table = jnp.concatenate(
        [coords.reshape(3, leaves, width), (weights.reshape(leaves, width) * alive)[None]], axis=0
    )
    table = table.transpose(1, 0, 2)
    padded = padded_2(table, (("row", 0),), leaves)
    full = jnp.concatenate(
        [padded[leaves : 2 * leaves], padded[:leaves], padded[2 * leaves :]], axis=0
    )
    result = leaf_forces(full, table, sources, alive)
    return result.transpose(1, 0, 2).reshape(3, leaves * width)


def solution(mesh):
    return jax.shard_map(
        on_device,
        mesh=mesh,
        in_specs=(
            P(None, ("row", "col")),
            P(None, ("row", "col")),
            P(None, ("row", "col")),
            P(("row", "col"), None),
        ),
        out_specs=P(None, ("row", "col")),
        check_vma=False,
    )
```

profile of v0, /device:TPU:0, one launch (start us, length us, event | category | flops | bytes accessed | tf_op | source)
XLA Modules:
  0.0 44.4 jit_solution(10030716377979728203)
XLA Ops:
  0.0 0.6 %broadcast.80 = s32[]{:T(128)} broadcast(s32[]{:T(128)} %copy.43), dimensions={} | broadcast | bytes 8 | tf_op args[2]
  0.6 1.4 %reduce.8 = s32[16]{0:T(128)S(1)} reduce(s32[1,16]{1,0:T(1,128)} %param.8, s32[]{:T(128)} %broadcast.80), dimensions={0}, to_apply=%param.8.reduce_sub_computation.3 | reduce | bytes 132 | tf_op args[2]
  2.0 0.1 all_to_all.20
  2.0 9.7 %all_to_all.27 = s32[1,8,2]{2,0,1:T(1,128)S(1)} all-to-all(s32[1,8,2]{2,0,1:T(1,128)S(1)} %bitcast.86), channel_id=1, replica_groups=mesh['row'=4,'col'=8] {'col'}, dimensions={1} | all-to-all | bytes 128 | tf_op jit(solution)/shard_map/all_to_all | solution.py:50
  11.7 3.3 %all-to-all-start.2 = ((f32[1,8,256]{2,0,1:T(1,128)}), f32[1,8,256]{2,0,1:T(1,128)S(1)}, u32[]{:S(2)}, u32[]{:S(2)}) async-start(f32[1,8,256]{2,0,1:T(1,128)} %bitcast.87), calls=%async_computation.2 | async-start | bytes 16384 | tf_op jit(solution)/shard_map/all_to_all | solution.py:49
  15.1 0.8 %copy.28 = s32[16,8]{1,0:T(8,128)S(1)} copy(s32[16,8]{0,1:T(8,128)} %param.9) | data formatting | bytes 1024 | tf_op jit(solution)/shard_map/while | solution.py:42
  15.8 0.7 %reduce.9 = s32[8,2]{1,0:T(8,128)S(1)} reduce(s32[1,8,2]{2,0,1:T(1,128)S(1)} %all_to_all.27, s32[]{:T(128)} %broadcast.80), dimensions={0}, to_apply=%all_to_all.21.reduce_sub_computation.5 | reduce | bytes 132 | tf_op jit(solution)/shard_map/all_to_all | solution.py:50
  16.5 0.1 lt.37
  16.7 3.0 %all-to-all-done.2 = f32[1,8,256]{2,0,1:T(1,128)S(1)} async-done(((f32[1,8,256]{2,0,1:T(1,128)}), f32[1,8,256]{2,0,1:T(1,128)S(1)}, u32[]{:S(2)}, u32[]{:S(2)}) %all-to-all-start.2) | async-done | bytes 8224 | tf_op jit(solution)/shard_map/all_to_all | solution.py:49
  19.7 3.3 %all-to-all-start = ((f32[3,8,256]{2,0,1:T(4,128)}), f32[3,8,256]{2,0,1:T(4,128)S(1)}, u32[]{:S(2)}, u32[]{:S(2)}) async-start(f32[3,8,256]{2,0,1:T(4,128)} %bitcast.83), calls=%async_computation | async-start | bytes 65536 | tf_op jit(solution)/shard_map/all_to_all | solution.py:48
  23.1 4.7 %all-to-all-done = f32[3,8,256]{2,0,1:T(4,128)S(1)} async-done(((f32[3,8,256]{2,0,1:T(4,128)}), f32[3,8,256]{2,0,1:T(4,128)S(1)}, u32[]{:S(2)}, u32[]{:S(2)}) %all-to-all-start) | async-done | bytes 24608 | tf_op jit(solution)/shard_map/all_to_all | solution.py:48
  27.8 1.6 %collective-permute-start = (f32[16,4,128]{2,0,1:T(8,128)S(1)}, f32[16,4,128]{2,0,1:T(8,128)S(1)}, u32[]{:S(2)}, u32[]{:S(2)}) collective-permute-start(f32[16,4,128]{2,0,1:T(8,128)S(1)} %get-tuple-element.91), channel_id=1, source_target_pairs={{0,8},{8,16},{16,24},{24,0},{1,9},{9,17},{17,25},{25,1},{2,10},{10... | collective-permute-start | bytes 98312 | tf_op jit(solution)/shard_map/ppermute | solution.py:16
  29.5 2.2 %collective-permute-start.1 = (f32[16,4,128]{2,0,1:T(8,128)S(1)}, f32[16,4,128]{2,0,1:T(8,128)S(1)}, u32[]{:S(2)}, u32[]{:S(2)}) collective-permute-start(f32[16,4,128]{2,0,1:T(8,128)S(1)} %get-tuple-element.91), channel_id=1, source_target_pairs={{8,0},{16,8},{24,16},{0,24},{9,1},{17,9},{25,17},{1,25},{10,2},{18... | collective-permute-start | bytes 98312 | tf_op jit(solution)/shard_map/ppermute | solution.py:17
  31.8 1.9 %collective-permute-done = f32[16,4,128]{2,0,1:T(8,128)S(1)} collective-permute-done((f32[16,4,128]{2,0,1:T(8,128)S(1)}, f32[16,4,128]{2,0,1:T(8,128)S(1)}, u32[]{:S(2)}, u32[]{:S(2)}) %collective-permute-start) | collective-permute-done | bytes 32800 | tf_op jit(solution)/shard_map/ppermute | solution.py:16
  33.8 10.0 %while.10 = (s32[]{:T(128)}, f32[2,8,3,128]{3,1,0,2:T(8,128)S(1)}, s32[2,8,8]{2,1,0:T(8,128)S(1)}, f32[48,4,128]{2,1,0:T(4,128)S(1)}, f32[2,8,4,128]{3,1,0,2:T(8,128)S(1)}, /*index=5*/f32[2,8,128]{2,1,0:T(8,128)S(1)}, s32[]{:T(128)}) while((s32[]{:T(128)}, f32[2,8,3,128]{3,1,0,2:T(8,128)S(1)}, s32[2,8,8]{2,1,0:T(8,128)S(1)}, ...), condition=%wide.region_4.5_spmd, body=%wide.region_0.4_spmd.sunk | while | flops 17833152 | bytes 779869 | solution.py:42
  33.8 0.1 reshape.198
  33.9 0.7 %gather_fusion = f32[64,4,128]{2,1,0:T(4,128)S(1)} fusion(f32[48,4,128]{2,1,0:T(4,128)S(1)} %get-tuple-element.166, s32[1024]{0:T(1024)S(1)} %pad_clamp_fusion.2), kind=kCustom, calls=%fused_computation.clone.1 | custom fusion | bytes 262400 | tf_op jit(solution)/shard_map/while/body/eval_jaxpr/gather | solution.py:31
  34.6 0.1 fusion.17
  34.7 4.0 %fusion.18 = (f32[8,128]{1,0:T(8,128)S(1)}, f32[8,128]{1,0:T(8,128)S(1)}, f32[8,128]{1,0:T(8,128)S(1)}) fusion(f32[8,128]{1,0:T(8,128)S(1)} %get-tuple-element.139, f32[8,8,128]{2,1,0:T(8,128)S(1)} %bitcast.76, f32[8,128]{1,0:T(8,128)S(1)} %get-tuple-element.141, f32[8,8,128]{2,1,0:T(8,128)S(1)} %bitcast.77, f32[8,128]{1,0:T(8,128)S(1)} %get-tuple-element.143, ...), kind=kLoop, calls=%fused_computation.11.clone.1 | loop fusion | flops 17822720 | bytes 155648 | tf_op jit(solution)/shard_map/while/body/eval_jaxpr/reduce_sum | solution.py:37
  38.8 0.1 reshape.198
  38.9 0.7 %gather_fusion = f32[64,4,128]{2,1,0:T(4,128)S(1)} fusion(f32[48,4,128]{2,1,0:T(4,128)S(1)} %get-tuple-element.166, s32[1024]{0:T(1024)S(1)} %pad_clamp_fusion.2), kind=kCustom, calls=%fused_computation.clone.1 | custom fusion | bytes 262400 | tf_op jit(solution)/shard_map/while/body/eval_jaxpr/gather | solution.py:31
  39.6 0.1 fusion.17
  39.7 4.0 %fusion.18 = (f32[8,128]{1,0:T(8,128)S(1)}, f32[8,128]{1,0:T(8,128)S(1)}, f32[8,128]{1,0:T(8,128)S(1)}) fusion(f32[8,128]{1,0:T(8,128)S(1)} %get-tuple-element.139, f32[8,8,128]{2,1,0:T(8,128)S(1)} %bitcast.76, f32[8,128]{1,0:T(8,128)S(1)} %get-tuple-element.141, f32[8,8,128]{2,1,0:T(8,128)S(1)} %bitcast.77, f32[8,128]{1,0:T(8,128)S(1)} %get-tuple-element.143, ...), kind=kLoop, calls=%fused_computation.11.clone.1 | loop fusion | flops 17822720 | bytes 155648 | tf_op jit(solution)/shard_map/while/body/eval_jaxpr/reduce_sum | solution.py:37
  43.8 0.6 %copy.34 = f32[1,3,16,128]{3,1,2,0:T(4,128)} copy(f32[1,3,16,128]{3,2,1,0:T(8,128)S(1)} %bitcast.85) | data formatting | bytes 49152
  (22 shorter events, 0.4 us)
Async XLA Ops:
  11.7 8.0 %all-to-all-start.2 = ((f32[1,8,256]{2,0,1:T(1,128)}), f32[1,8,256]{2,0,1:T(1,128)S(1)}, u32[]{:S(2)}, u32[]{:S(2)}) async-start(f32[1,8,256]{2,0,1:T(1,128)} %bitcast.87), calls=%async_computation.2 | async-start | bytes 16384 | tf_op jit(solution)/shard_map/all_to_all | solution.py:49
  19.7 8.1 %all-to-all-start = ((f32[3,8,256]{2,0,1:T(4,128)}), f32[3,8,256]{2,0,1:T(4,128)S(1)}, u32[]{:S(2)}, u32[]{:S(2)}) async-start(f32[3,8,256]{2,0,1:T(4,128)} %bitcast.83), calls=%async_computation | async-start | bytes 65536 | tf_op jit(solution)/shard_map/all_to_all | solution.py:48
  27.8 5.9 %collective-permute-start = (f32[16,4,128]{2,0,1:T(8,128)S(1)}, f32[16,4,128]{2,0,1:T(8,128)S(1)}, u32[]{:S(2)}, u32[]{:S(2)}) collective-permute-start(f32[16,4,128]{2,0,1:T(8,128)S(1)} %get-tuple-element.91), channel_id=1, source_target_pairs={{0,8},{8,16},{16,24},{24,0},{1,9},{9,17},{17,25},{25,1},{2,10},{10... | collective-permute-start | bytes 98312 | tf_op jit(solution)/shard_map/ppermute | solution.py:16
  29.5 4.3 %collective-permute-start.1 = (f32[16,4,128]{2,0,1:T(8,128)S(1)}, f32[16,4,128]{2,0,1:T(8,128)S(1)}, u32[]{:S(2)}, u32[]{:S(2)}) collective-permute-start(f32[16,4,128]{2,0,1:T(8,128)S(1)} %get-tuple-element.91), channel_id=1, source_target_pairs={{8,0},{16,8},{24,16},{0,24},{9,1},{17,9},{25,17},{1,25},{10,2},{18... | collective-permute-start | bytes 98312 | tf_op jit(solution)/shard_map/ppermute | solution.py:17
where the time goes:
time: 44.8 us; the launch traced here: 44.4 us
  starting transfers between devices  10.6 us (24%)
  other arithmetic  10.4 us (23%)
  blocking collectives  9.68 us (22%)
  waiting for transfers between devices  9.65 us (22%)
  local copies, waits for them, and re-layouts  3.98 us (9%)
    all_to_all x1, blocking collectives, on_device(): lax.all_to_all(counts, 'col', split_axis=1, concat_axis=1, tiled=True)  9.68 us
    reduce_sum x2, other arithmetic, one_group(): pull_x = jnp.sum(weight * delta_x, axis=(1, 3))  8.08 us
    all_to_all x1, waiting for transfers between devices, on_device(): lax.all_to_all(positions, 'col', split_axis=1, concat_axis=1, tiled=True)  4.7 us
    all_to_all x1, starting transfers between devices, on_device(): lax.all_to_all(positions, 'col', split_axis=1, concat_axis=1, tiled=True)  3.34 us
    all_to_all x1, starting transfers between devices, on_device(): lax.all_to_all(masses, 'col', split_axis=1, concat_axis=1, tiled=True)  3.33 us
    all_to_all x1, waiting for transfers between devices, on_device(): lax.all_to_all(masses, 'col', split_axis=1, concat_axis=1, tiled=True)  3 us
    ppermute x1, starting transfers between devices, padded_2(): after = lax.ppermute(leading, axis, down)  2.25 us
    ppermute x1, waiting for transfers between devices, padded_2(): before = lax.ppermute(last, axis, up)  1.92 us
  transfers between devices with their start and end apart: 4, of which 3 were waited for; matrix products, arithmetic and copies ran while one was open for 4% of the time, Pallas kernels for 0%

commit v1 on v0

--- a/solution.py
+++ b/solution.py
@@ -4,6 +4,12 @@
 from jax.sharding import PartitionSpec as P
 
 softening = 2.5e-07
+
+
+def stacked_exchange(x, mesh_axis, split, join):
+    pieces = jnp.split(x, lax.axis_size(mesh_axis), axis=split)
+    incoming = lax.all_to_all(jnp.stack(pieces), mesh_axis, 0, 0)
+    return jnp.concatenate(incoming, axis=join)
 
 
 def padded_2(shard, sides, width):
@@ -45,7 +51,7 @@
 
 def on_device(positions, masses, counts, sources):
     coords, weights, livecount = (
-        lax.all_to_all(positions, "col", split_axis=1, concat_axis=1, tiled=True),
+        stacked_exchange(positions, "col", 1, 1),
         lax.all_to_all(masses, "col", split_axis=1, concat_axis=1, tiled=True),
         lax.all_to_all(counts, "col", split_axis=1, concat_axis=1, tiled=True),
     )

time: 44.8 us -> 50.9 us (1.14)
  local copies, waits for them, and re-layouts: 3.98 us -> 14.8 us
  blocking collectives: 9.68 us -> 0 us
  starting transfers between devices: 10.6 us -> 16.6 us
  waiting for transfers between devices: 9.65 us -> 8.51 us
    all_to_all x1 -> x0, blocking collectives: 9.68 us -> none  [on_device(): lax.all_to_all(counts, 'col', split_axis=1, concat_axis=1, tiled=True)]
    unnamed x2 -> x9, local copies, waits for them, and re-layouts: 1.22 us -> 10.1 us
    all_to_all x1 -> x2, starting transfers between devices: 3.34 us -> 8.54 us  [the longest x1 5.2 us: on_device(): lax.all_to_all(counts, 'col', split_axis=1, concat_axis=1, tiled=True)]
    another operation x0 -> x2, local copies, waits for them, and re-layouts: none -> 1.28 us  [the longest x1 1.28 us: stacked_exchange(): incoming = lax.all_to_all(jnp.stack(pieces), mesh_axis, 0, 0)]
    all_to_all x1, waiting for transfers between devices: 3 us -> 1.86 us  [on_device(): lax.all_to_all(masses, 'col', split_axis=1, concat_axis=1, tiled=True)]
    all_to_all x1, starting transfers between devices: 3.33 us -> 4.2 us  [on_device(): lax.all_to_all(masses, 'col', split_axis=1, concat_axis=1, tiled=True)]
    all_to_all x1, local copies, waits for them, and re-layouts: 0.08 us -> 0.68 us  [on_device(): lax.all_to_all(counts, 'col', split_axis=1, concat_axis=1, tiled=True)]
    all_to_all x1 -> x2, waiting for transfers between devices: 4.7 us -> 4.7 us  [the longest x1 4.7 us: stacked_exchange(): incoming = lax.all_to_all(jnp.stack(pieces), mesh_axis, 0, 0)]
  transfers between devices with their start and end apart: 4 -> 5, of which waited for: 3 -> 3; matrix products, arithmetic and copies ran while one was open for 4% -> 24% of each run, Pallas kernels for 0% -> 0%
where the time goes in v1:
time: 50.9 us; the launch traced here: 50.3 us
  starting transfers between devices  16.6 us (33%)
  local copies, waits for them, and re-layouts  14.8 us (29%)
  other arithmetic  10.2 us (20%)
  waiting for transfers between devices  8.51 us (17%)
    unnamed x9, local copies, waits for them, and re-layouts  10.1 us
    reduce_sum x2, other arithmetic, one_group(): pull_x = jnp.sum(weight * delta_x, axis=(1, 3))  8 us
    all_to_all x1, starting transfers between devices, on_device(): lax.all_to_all(counts, 'col', split_axis=1, concat_axis=1, tiled=True)  5.2 us
    all_to_all x1, waiting for transfers between devices, stacked_exchange(): incoming = lax.all_to_all(jnp.stack(pieces), mesh_axis, 0, 0)  4.7 us
    all_to_all x1, starting transfers between devices, on_device(): lax.all_to_all(masses, 'col', split_axis=1, concat_axis=1, tiled=True)  4.2 us
    all_to_all x1, starting transfers between devices, stacked_exchange(): incoming = lax.all_to_all(jnp.stack(pieces), mesh_axis, 0, 0)  3.34 us
    ppermute x1, starting transfers between devices, padded_2(): after = lax.ppermute(leading, axis, down)  2.25 us
    ppermute x1, waiting for transfers between devices, padded_2(): before = lax.ppermute(last, axis, up)  1.92 us
  transfers between devices with their start and end apart: 5, of which 3 were waited for; matrix products, arithmetic and copies ran while one was open for 24% of the time, Pallas kernels for 0%

profile of v1, /device:TPU:0, one launch (start us, length us, event | category | flops | bytes accessed | tf_op | source)
XLA Modules:
  0.0 50.3 jit_solution(13343203345484556276)
XLA Ops:
  0.5 1.3 %reduce.8 = s32[16]{0:T(128)S(1)} reduce(s32[1,16]{1,0:T(1,128)} %param.8, s32[]{:T(128)} %broadcast.80), dimensions={0}, to_apply=%param.8.reduce_sub_computation.3 | reduce | bytes 132 | tf_op args[2]
  1.8 0.7 %all_to_all.16 = s32[1,8,2]{2,1,0:T(8,128)} reshape(s32[16]{0:T(128)S(1)} %reduce.8) | data formatting | bytes 128 | tf_op jit(solution)/shard_map/all_to_all | solution.py:56
  2.5 5.2 %all-to-all-start.1 = ((s32[1,8,2]{2,0,1:T(1,128)}), s32[1,8,2]{2,0,1:T(1,128)S(1)}, u32[]{:S(2)}, u32[]{:S(2)}) async-start(s32[1,8,2]{2,0,1:T(1,128)} %bitcast.24), calls=%async_computation.1 | async-start | bytes 8192 | tf_op jit(solution)/shard_map/all_to_all | solution.py:56
  7.7 1.3 %constant_dynamic-update-slice_fusion.7 = f32[8,3,256]{2,1,0:T(4,128)} fusion(f32[3,2048]{1,0:T(4,128)} %param.6), kind=kLoop, calls=%fused_computation.37 | loop fusion | bytes 7168
  9.0 1.3 %constant_dynamic-update-slice_fusion.6 = f32[8,3,256]{2,1,0:T(4,128)} fusion(f32[8,3,256]{2,1,0:T(4,128)} %constant_dynamic-update-slice_fusion.7, f32[3,2048]{1,0:T(4,128)} %param.6), kind=kLoop, calls=%fused_computation.36 | loop fusion | bytes 8192
  10.3 1.3 %constant_dynamic-update-slice_fusion.5 = f32[8,3,256]{2,1,0:T(4,128)} fusion(f32[8,3,256]{2,1,0:T(4,128)} %constant_dynamic-update-slice_fusion.6, f32[3,2048]{1,0:T(4,128)} %param.6), kind=kLoop, calls=%fused_computation.35 | loop fusion | bytes 8192
  11.6 1.3 %constant_dynamic-update-slice_fusion.4 = f32[8,3,256]{2,1,0:T(4,128)} fusion(f32[8,3,256]{2,1,0:T(4,128)} %constant_dynamic-update-slice_fusion.5, f32[3,2048]{1,0:T(4,128)} %param.6), kind=kLoop, calls=%fused_computation.34 | loop fusion | bytes 8192
  12.8 1.3 %constant_dynamic-update-slice_fusion.3 = f32[8,3,256]{2,1,0:T(4,128)} fusion(f32[8,3,256]{2,1,0:T(4,128)} %constant_dynamic-update-slice_fusion.4, f32[3,2048]{1,0:T(4,128)} %param.6), kind=kLoop, calls=%fused_computation.33 | loop fusion | bytes 8192
  14.1 1.3 %constant_dynamic-update-slice_fusion.2 = f32[8,3,256]{2,1,0:T(4,128)} fusion(f32[8,3,256]{2,1,0:T(4,128)} %constant_dynamic-update-slice_fusion.3, f32[3,2048]{1,0:T(4,128)} %param.6), kind=kLoop, calls=%fused_computation.32 | loop fusion | bytes 8192
  15.4 1.3 %constant_dynamic-update-slice_fusion.1 = f32[8,3,256]{2,1,0:T(4,128)} fusion(f32[8,3,256]{2,1,0:T(4,128)} %constant_dynamic-update-slice_fusion.2, f32[3,2048]{1,0:T(4,128)} %param.6), kind=kLoop, calls=%fused_computation.31 | loop fusion | bytes 8192
  16.7 4.2 %all-to-all-start.2 = ((f32[1,8,256]{2,0,1:T(1,128)}), f32[1,8,256]{2,0,1:T(1,128)S(1)}, u32[]{:S(2)}, u32[]{:S(2)}) async-start(f32[1,8,256]{2,0,1:T(1,128)} %bitcast.102), calls=%async_computation.2 | async-start | bytes 16384 | tf_op jit(solution)/shard_map/all_to_all | solution.py:55
  20.9 1.3 %constant_dynamic-update-slice_fusion = f32[8,3,256]{2,1,0:T(4,128)} fusion(f32[8,3,256]{2,1,0:T(4,128)} %constant_dynamic-update-slice_fusion.1, f32[3,2048]{1,0:T(4,128)} %param.6), kind=kLoop, calls=%fused_computation.30 | loop fusion | bytes 8192 | tf_op jit(solution)/shard_map/stack | solution.py:11
  22.2 0.8 %copy.22 = s32[16,8]{1,0:T(8,128)S(1)} copy(s32[16,8]{0,1:T(8,128)} %param.9) | data formatting | bytes 1024 | tf_op jit(solution)/shard_map/while | solution.py:48
  23.7 1.9 %all-to-all-done.2 = f32[1,8,256]{2,0,1:T(1,128)S(1)} async-done(((f32[1,8,256]{2,0,1:T(1,128)}), f32[1,8,256]{2,0,1:T(1,128)S(1)}, u32[]{:S(2)}, u32[]{:S(2)}) %all-to-all-start.2) | async-done | bytes 8224 | tf_op jit(solution)/shard_map/all_to_all | solution.py:55
  25.6 3.3 %all-to-all-start = ((f32[8,3,256]{2,1,0:T(4,128)}), f32[8,3,256]{2,1,0:T(4,128)S(1)}, u32[]{:S(2)}, u32[]{:S(2)}) async-start(f32[8,3,256]{2,1,0:T(4,128)} %constant_dynamic-update-slice_fusion), calls=%async_computation | async-start | bytes 65536 | tf_op jit(solution)/shard_map/all_to_all | solution.py:11
  29.0 4.7 %all-to-all-done = f32[8,3,256]{2,1,0:T(4,128)S(1)} async-done(((f32[8,3,256]{2,1,0:T(4,128)}), f32[8,3,256]{2,1,0:T(4,128)S(1)}, u32[]{:S(2)}, u32[]{:S(2)}) %all-to-all-start) | async-done | bytes 24608 | tf_op jit(solution)/shard_map/all_to_all | solution.py:11
  33.7 1.6 %collective-permute-start = (f32[16,4,128]{2,0,1:T(8,128)S(1)}, f32[16,4,128]{2,0,1:T(8,128)S(1)}, u32[]{:S(2)}, u32[]{:S(2)}) collective-permute-start(f32[16,4,128]{2,0,1:T(8,128)S(1)} %get-tuple-element.91), channel_id=1, source_target_pairs={{0,8},{8,16},{16,24},{24,0},{1,9},{9,17},{17,25},{25,1},{2,10},{10... | collective-permute-start | bytes 98312 | tf_op jit(solution)/shard_map/ppermute | solution.py:22
  35.4 2.2 %collective-permute-start.1 = (f32[16,4,128]{2,0,1:T(8,128)S(1)}, f32[16,4,128]{2,0,1:T(8,128)S(1)}, u32[]{:S(2)}, u32[]{:S(2)}) collective-permute-start(f32[16,4,128]{2,0,1:T(8,128)S(1)} %get-tuple-element.91), channel_id=1, source_target_pairs={{8,0},{16,8},{24,16},{0,24},{9,1},{17,9},{25,17},{1,25},{10,2},{18... | collective-permute-start | bytes 98312 | tf_op jit(solution)/shard_map/ppermute | solution.py:23
  37.7 1.9 %collective-permute-done = f32[16,4,128]{2,0,1:T(8,128)S(1)} collective-permute-done((f32[16,4,128]{2,0,1:T(8,128)S(1)}, f32[16,4,128]{2,0,1:T(8,128)S(1)}, u32[]{:S(2)}, u32[]{:S(2)}) %collective-permute-start) | collective-permute-done | bytes 32800 | tf_op jit(solution)/shard_map/ppermute | solution.py:22
  39.7 9.9 %while.10 = (s32[]{:T(128)}, f32[2,8,3,128]{3,1,0,2:T(8,128)S(1)}, s32[2,8,8]{2,1,0:T(8,128)S(1)}, f32[48,4,128]{2,1,0:T(4,128)S(1)}, f32[2,8,4,128]{3,1,0,2:T(8,128)S(1)}, /*index=5*/f32[2,8,128]{2,1,0:T(8,128)S(1)}, s32[]{:T(128)}) while((s32[]{:T(128)}, f32[2,8,3,128]{3,1,0,2:T(8,128)S(1)}, s32[2,8,8]{2,1,0:T(8,128)S(1)}, ...), condition=%wide.region_4.5_spmd, body=%wide.region_0.4_spmd.sunk | while | flops 17833152 | bytes 779869 | solution.py:48
  39.8 0.7 %gather_fusion = f32[64,4,128]{2,1,0:T(4,128)S(1)} fusion(f32[48,4,128]{2,1,0:T(4,128)S(1)} %get-tuple-element.166, s32[1024]{0:T(1024)S(1)} %pad_clamp_fusion.2), kind=kCustom, calls=%fused_computation.clone.1 | custom fusion | bytes 262400 | tf_op jit(solution)/shard_map/while/body/eval_jaxpr/gather | solution.py:37
  40.6 4.0 %fusion.18 = (f32[8,128]{1,0:T(8,128)S(1)}, f32[8,128]{1,0:T(8,128)S(1)}, f32[8,128]{1,0:T(8,128)S(1)}) fusion(f32[8,128]{1,0:T(8,128)S(1)} %get-tuple-element.139, f32[8,8,128]{2,1,0:T(8,128)S(1)} %bitcast.92, f32[8,128]{1,0:T(8,128)S(1)} %get-tuple-element.141, f32[8,8,128]{2,1,0:T(8,128)S(1)} %bitcast.93, f32[8,128]{1,0:T(8,128)S(1)} %get-tuple-element.143, ...), kind=kLoop, calls=%fused_computation.11.clone.1 | loop fusion | flops 17822720 | bytes 155648 | tf_op jit(solution)/shard_map/while/body/eval_jaxpr/reduce_sum | solution.py:43
  44.8 0.7 %gather_fusion = f32[64,4,128]{2,1,0:T(4,128)S(1)} fusion(f32[48,4,128]{2,1,0:T(4,128)S(1)} %get-tuple-element.166, s32[1024]{0:T(1024)S(1)} %pad_clamp_fusion.2), kind=kCustom, calls=%fused_computation.clone.1 | custom fusion | bytes 262400 | tf_op jit(solution)/shard_map/while/body/eval_jaxpr/gather | solution.py:37
  45.6 4.0 %fusion.18 = (f32[8,128]{1,0:T(8,128)S(1)}, f32[8,128]{1,0:T(8,128)S(1)}, f32[8,128]{1,0:T(8,128)S(1)}) fusion(f32[8,128]{1,0:T(8,128)S(1)} %get-tuple-element.139, f32[8,8,128]{2,1,0:T(8,128)S(1)} %bitcast.92, f32[8,128]{1,0:T(8,128)S(1)} %get-tuple-element.141, f32[8,8,128]{2,1,0:T(8,128)S(1)} %bitcast.93, f32[8,128]{1,0:T(8,128)S(1)} %get-tuple-element.143, ...), kind=kLoop, calls=%fused_computation.11.clone.1 | loop fusion | flops 17822720 | bytes 155648 | tf_op jit(solution)/shard_map/while/body/eval_jaxpr/reduce_sum | solution.py:43
  (31 shorter events, 2.7 us)
Async XLA Ops:
  2.5 14.2 %all-to-all-start.1 = ((s32[1,8,2]{2,0,1:T(1,128)}), s32[1,8,2]{2,0,1:T(1,128)S(1)}, u32[]{:S(2)}, u32[]{:S(2)}) async-start(s32[1,8,2]{2,0,1:T(1,128)} %bitcast.24), calls=%async_computation.1 | async-start | bytes 8192 | tf_op jit(solution)/shard_map/all_to_all | solution.py:56
  16.7 8.9 %all-to-all-start.2 = ((f32[1,8,256]{2,0,1:T(1,128)}), f32[1,8,256]{2,0,1:T(1,128)S(1)}, u32[]{:S(2)}, u32[]{:S(2)}) async-start(f32[1,8,256]{2,0,1:T(1,128)} %bitcast.102), calls=%async_computation.2 | async-start | bytes 16384 | tf_op jit(solution)/shard_map/all_to_all | solution.py:55
  25.6 8.1 %all-to-all-start = ((f32[8,3,256]{2,1,0:T(4,128)}), f32[8,3,256]{2,1,0:T(4,128)S(1)}, u32[]{:S(2)}, u32[]{:S(2)}) async-start(f32[8,3,256]{2,1,0:T(4,128)} %constant_dynamic-update-slice_fusion), calls=%async_computation | async-start | bytes 65536 | tf_op jit(solution)/shard_map/all_to_all | solution.py:11
  33.7 5.9 %collective-permute-start = (f32[16,4,128]{2,0,1:T(8,128)S(1)}, f32[16,4,128]{2,0,1:T(8,128)S(1)}, u32[]{:S(2)}, u32[]{:S(2)}) collective-permute-start(f32[16,4,128]{2,0,1:T(8,128)S(1)} %get-tuple-element.91), channel_id=1, source_target_pairs={{0,8},{8,16},{16,24},{24,0},{1,9},{9,17},{17,25},{25,1},{2,10},{10... | collective-permute-start | bytes 98312 | tf_op jit(solution)/shard_map/ppermute | solution.py:22
  35.4 4.3 %collective-permute-start.1 = (f32[16,4,128]{2,0,1:T(8,128)S(1)}, f32[16,4,128]{2,0,1:T(8,128)S(1)}, u32[]{:S(2)}, u32[]{:S(2)}) collective-permute-start(f32[16,4,128]{2,0,1:T(8,128)S(1)} %get-tuple-element.91), channel_id=1, source_target_pairs={{8,0},{16,8},{24,16},{0,24},{9,1},{17,9},{25,17},{1,25},{10,2},{18... | collective-permute-start | bytes 98312 | tf_op jit(solution)/shard_map/ppermute | solution.py:23
